TPU v7x, 256 devices: a whole 4x4x8 slice. The times are simulated.
256 devices in a mesh: cuts: 16 (over z_lo, y, core), col: 16 (over z_hi, x).
Axes of the slice: x: 4, y: 4, z: 8 (z_hi: 4, z_lo: 2; z = z_hi * 2 + z_lo), core: 2. Of those that a mesh axis runs over, the one named last changes fastest.
Arguments:
- data: bfloat16 [16, 64, 64, 1024], P('cuts', None, 'col'), may hold values from -12 to 12
- weights: float32 [16, 64], replicated, may hold values from 0.5 to 2
- mixing: float32 [64, 64], replicated, may hold values from -0.4 to 2.9
Outputs:
- factor: float32 [64, 64, 1024], P(None, 'col')
- updated: float32 [16, 64], P('cuts')
All inputs are finite; a program needn't handle non-finite values.
Results may differ from a plain program's by a relative error of at most 0.0029.
Values sent between devices are 32-bit elements; how exact they have to be, the bound alone decides.
A program may use at most 64 MiB of HBM per device.

v0:
```python
import jax
import jax.numpy as jnp
from jax import lax
from jax.sharding import PartitionSpec as P

GRID = 32
ITERS = 3
strength = 0.5
highest = lax.Precision.HIGHEST
low_edge = 1.0
high_edge = 1.0 + 12.0 * strength
centre = (high_edge + low_edge) / 2.0
spread = (high_edge - low_edge) / 2.0


def extended_2(cells, sides, width):
    for axis, dim in sides:
        count = lax.axis_size(axis)
        ends = count - 1
        head = lax.slice_in_dim(cells, 0, width, axis=dim)
        tail = lax.slice_in_dim(cells, cells.shape[dim] - width, cells.shape[dim], axis=dim)
        cells = jnp.concatenate(
            [
                lax.ppermute(tail, axis, [(i, (i + 1) % count) for i in range(ends)]),
                cells,
                lax.ppermute(head, axis, [((i + 1) % count, i) for i in range(ends)]),
            ],
            axis=dim,
        )
    return cells


def split_up(shard, dim, devices):
    before, after = (shard.shape[:dim], shard.shape[dim + 1 :])
    return jnp.moveaxis(shard.reshape(*before, devices, -1, *after), dim, 0)


def sent_and_summed(shard, axis, dim):
    tiles = split_up(shard, dim, lax.axis_size(axis))
    arrived = lax.all_to_all(tiles, axis, split_axis=0, concat_axis=0, tiled=True)
    return arrived.sum(axis=0)


def joined_along(tiles, dim):
    dims = list(tiles.shape[1:])
    dims[dim] *= tiles.shape[0]
    return jnp.moveaxis(tiles, 0, dim).reshape(dims)


def from_everyone(shard, axis):
    devices = lax.axis_size(axis)
    return lax.all_to_all(
        jnp.broadcast_to(shard[None], (devices, *shard.shape)), axis, 0, 0, tiled=True
    )


def gather_directly(shard, axis, dim):
    return joined_along(from_everyone(shard, axis), dim)


def taken_together(shard, axis):
    return from_everyone(shard, axis).sum(axis=0)


def packed_total(arrays, axis):
    line, at, done = (jnp.concatenate([a.reshape(-1) for a in arrays]), 0, [])
    running = taken_together(line, axis)
    for a in arrays:
        done.append(running[at : at + a.size].reshape(a.shape))
        at += a.size
    return tuple(done)


def operate(extended):
    channels, depth, cells = extended.shape
    edge = GRID
    interior = extended[:, 1:-1]
    column = jnp.arange(cells, dtype=jnp.int32) % edge
    has_left = (column > 0).astype(jnp.float32)
    has_right = (column < edge - 1).astype(jnp.float32)
    left_part = jnp.pad(interior, ((0, 0), (0, 0), (1, 0)))[:, :, :-1] * has_left
    right_part = jnp.pad(interior, ((0, 0), (0, 0), (0, 1)))[:, :, 1:] * has_right
    upper_part = jnp.pad(interior, ((0, 0), (0, 0), (edge, 0)))[:, :, :-edge]
    lower_part = jnp.pad(interior, ((0, 0), (0, 0), (0, edge)))[:, :, edge:]
    neighbours = extended[:, 2:] + extended[:, :-2]
    neighbours = neighbours + left_part + right_part + upper_part + lower_part
    return interior + strength * (6.0 * interior - neighbours)


def smooth_once(source):
    planes = source.shape[1]
    extended = extended_2(source, (("col", 1),), ITERS)
    first_plane = lax.axis_index("col") * planes - ITERS
    total_planes = planes * lax.axis_size("col")
    levels = first_plane + jnp.arange(planes + 2 * ITERS, dtype=jnp.int32)
    inside = ((levels >= 0) & (levels < total_planes)).astype(jnp.float32)[None, :, None]
    solution = jnp.zeros_like(source)
    residual = extended
    direction = extended / centre
    ratio = spread / centre
    for iteration in range(ITERS):
        margin = ITERS - iteration
        solution = solution + direction[:, margin : margin + planes]
        window = inside[:, iteration + 1 : iteration + 1 + planes + 2 * (margin - 1)]
        residual = (residual[:, 1:-1] - operate(direction)) * window
        ratio_next = 1.0 / (2.0 * centre / spread - ratio)
        direction = ratio_next * ratio * direction[:, 1:-1] + 2.0 * ratio_next / spread * residual
        ratio = ratio_next
    return solution + direction


def smooth(source):
    return smooth_once(source)


def per_device(data, weights, mixing):
    local_scans, ranks, planes, cells = data.shape
    mix_gram = jnp.dot(mixing.T, mixing, precision=highest)
    weight_gram = jnp.dot(weights.T, weights, precision=highest)
    lower_factor = jnp.linalg.cholesky(mix_gram * weight_gram)
    own_weights = lax.dynamic_slice_in_dim(
        weights, lax.axis_index("cuts") * local_scans, local_scans, 0
    )
    scaled = (mixing[None, :, :] * own_weights[:, None, :]).reshape(local_scans * ranks, ranks)
    coefficients = jax.scipy.linalg.cho_solve((lower_factor, True), scaled.T).T.astype(jnp.bfloat16)
    stacked = data.reshape(local_scans * ranks, planes * cells)
    portion = lax.psum_scatter(
        lax.dot_general(
            coefficients, stacked, (((0,), (0,)), ((), ())), preferred_element_type=jnp.float32
        ),
        "cuts",
        scatter_dimension=0,
        tiled=True,
    )
    smoothed = smooth(portion.reshape(-1, planes, cells))
    factor = lax.all_gather(smoothed, "cuts", axis=0, tiled=True)
    factor_flat = factor.reshape(ranks, planes * cells)
    factor_half = factor_flat.astype(jnp.bfloat16)
    factor_gram = jnp.dot(factor_flat, factor_flat.T, precision=highest)
    products = lax.dot_general(
        data.reshape(local_scans, ranks, planes * cells),
        factor_half,
        (((2,), (1,)), ((), ())),
        preferred_element_type=jnp.float32,
    )
    targets = jnp.sum(mixing[None, :, :] * products, axis=1)
    factor_gram, targets = lax.psum((factor_gram, targets), "col")
    lower_next = jnp.linalg.cholesky(mix_gram * factor_gram)
    updated = jax.scipy.linalg.cho_solve((lower_next, True), targets.T).T
    return (factor, updated)


def solution(mesh):
    return jax.shard_map(
        per_device,
        mesh=mesh,
        in_specs=(P("cuts", None, "col", None), P(), P()),
        out_specs=(P(None, "col", None), P("cuts", None)),
        check_vma=False,
    )
```

profile of v0, /device:TPU:8, one launch (start us, length us, event | category | flops | bytes accessed | tf_op | source)
XLA Modules:
  0.0 309.4 jit_solution(8941545026422105702)
XLA Ops:
  7.2 1.1 fusion.60
  8.7 5.8 %cholesky.44 = f32[64,64]{1,0:T(8,128)S(1)} custom-call(f32[64,64]{1,0:T(8,128)S(1)} %fusion.46), custom_call_target="Cholesky" | custom-call | tf_op jit(solution)/shard_map/jit(cholesky)/cholesky | solution.py:120
  14.5 0.6 compare_reduce_fusion.1
  15.2 0.7 fusion.37
  15.8 4.9 %custom-call.16 = f32[1,64,64]{1,2,0:T(8,128)S(1)} custom-call(f32[1,64,64]{2,1,0:T(8,128)S(1)} %fusion.37), custom_call_target="InvertDiagBlocksLowerTriangular" | custom-call | tf_op jit(solution)/shard_map/jit(_cho_solve)/triangular_solve | solution.py:125
  21.3 1.2 copy.38
  22.5 1.3 fusion.61
  23.9 0.7 copy-done.3
  26.0 122.3 %all-reduce.16.cloned.1.call-done = f32[64,4096]{1,0:T(8,128)} async-done(((f32[64,4096]{1,0:T(8,128)}), f32[64,4096]{1,0:T(8,128)}) %all-reduce.16.cloned.1.call-update) | async-done | bytes 1048592
  148.3 0.9 constant_dynamic-slice_fusion
  149.3 3.1 %collective-permute-start = (f32[4,3,1024]{2,1,0:T(4,128)S(1)}, f32[4,3,1024]{2,1,0:T(4,128)S(1)}, u32[]{:S(2)}, u32[]{:S(2)}) collective-permute-start(f32[4,3,1024]{2,1,0:T(4,128)S(1)} %get-tuple-element.15), channel_id=1, source_target_pairs={{0,1},{1,2},{2,3},{3,4},{4,5},{5,6},{6,7},{7,8},{8,9},{9,10},{10,1... | collective-permute-start | bytes 147464 | tf_op jit(solution)/shard_map/ppermute | solution.py:24
  152.4 1.3 collective-permute-start.1
  154.3 4.3 %collective-permute-done.1 = f32[4,3,1024]{2,1,0:T(4,128)S(1)} collective-permute-done((f32[4,3,1024]{2,1,0:T(4,128)S(1)}, f32[4,3,1024]{2,1,0:T(4,128)S(1)}, u32[]{:S(2)}, u32[]{:S(2)}) %collective-permute-start.1) | collective-permute-done | bytes 49184 | tf_op jit(solution)/shard_map/ppermute | solution.py:26
  159.2 0.9 fusion.36
  160.1 41.6 %all-gather.2.cloned.1.call-done = f32[64,4,1024]{2,1,0:T(4,128)} async-done(((f32[4,4,1024]{2,1,0:T(4,128)}), f32[64,4,1024]{2,1,0:T(4,128)}) %all-gather.2.cloned.1.call-update) | async-done | bytes 1048592 | tf_op jit(solution)/shard_map/all_gather | solution.py:136
  201.6 1.4 convert_element_type.73
  203.5 0.7 copy-done.1
  204.3 2.0 convolution_bitcast_fusion.1
  206.3 82.2 %all-reduce.13 = (f32[64,64]{0,1:T(8,128)S(1)}, f32[64]{0:T(128)S(1)}) all-reduce(f32[64,64]{0,1:T(8,128)S(1)} %convolution_bitcast_fusion.1, f32[64]{0:T(128)S(1)} %fusion.1), channel_id=1, replica_groups=mesh['cuts'=16,'col'=16] {'col'}, use_global_device_ids=true, to_apply=%region_3.5 | all-reduce | flops 4160 | bytes 33280 | tf_op jit(solution)/shard_map/psum | solution.py:147
  288.6 5.8 %cholesky.55 = f32[64,64]{1,0:T(8,128)S(1)} custom-call(f32[64,64]{1,0:T(8,128)S(1)} %fusion.42), custom_call_target="Cholesky" | custom-call | tf_op jit(solution)/shard_map/jit(cholesky)/cholesky | solution.py:148
  295.1 0.7 fusion.38
  295.8 4.9 %custom-call.17 = f32[1,64,64]{1,2,0:T(8,128)S(1)} custom-call(f32[1,64,64]{2,1,0:T(8,128)S(1)} %fusion.38), custom_call_target="InvertDiagBlocksLowerTriangular" | custom-call | tf_op jit(solution)/shard_map/jit(_cho_solve)/triangular_solve | solution.py:149
  300.9 0.7 fusion.39
  301.6 1.0 copy.44
  (40 shorter events, 4.4 us)
Async XLA Ops:
  7.2 1.1 copy-start
  7.2 141.1 %all-reduce.16.cloned.1.call-start = ((), (), s32[]{:S(2)}) async-start(), calls=%async_computation.1 | async-start | bytes 2097152
  15.2 5.6 %copy-start.2 = (f32[64,64]{1,0:T(8,128)S(1)}, f32[64,64]{1,0:T(8,128)}, u32[]{:S(2)}) copy-start(f32[64,64]{1,0:T(8,128)} %param.6) | copy-start | bytes 49156
  23.8 177.8 %all-gather.2.cloned.1.call-start = ((), (), s32[]{:S(2)}) async-start(), calls=%async_computation | async-start | bytes 1114112 | tf_op jit(solution)/shard_map/all_gather | solution.py:136
  23.8 0.7 copy-start.3
  149.3 5.0 %collective-permute-start = (f32[4,3,1024]{2,1,0:T(4,128)S(1)}, f32[4,3,1024]{2,1,0:T(4,128)S(1)}, u32[]{:S(2)}, u32[]{:S(2)}) collective-permute-start(f32[4,3,1024]{2,1,0:T(4,128)S(1)} %get-tuple-element.15), channel_id=1, source_target_pairs={{0,1},{1,2},{2,3},{3,4},{4,5},{5,6},{6,7},{7,8},{8,9},{9,10},{10,1... | collective-permute-start | bytes 147464 | tf_op jit(solution)/shard_map/ppermute | solution.py:24
  152.4 6.2 %collective-permute-start.1 = (f32[4,3,1024]{2,1,0:T(4,128)S(1)}, f32[4,3,1024]{2,1,0:T(4,128)S(1)}, u32[]{:S(2)}, u32[]{:S(2)}) collective-permute-start(f32[4,3,1024]{2,1,0:T(4,128)S(1)} %get-tuple-element.16), channel_id=1, source_target_pairs={{1,0},{2,1},{3,2},{4,3},{5,4},{6,5},{7,6},{8,7},{9,8},{10,9},{11,1... | collective-permute-start | bytes 147464 | tf_op jit(solution)/shard_map/ppermute | solution.py:26
  203.1 1.2 copy-start.1
Sparse Core Ops, SparseCore 0:
  23.9 124.2 all-reduce.15
  160.2 41.4 all-gather.1
where the time goes:
time: 310 us; the launch traced here: 309 us
  waiting for transfers between devices  169 us (55%)
  blocking collectives  82.2 us (27%)
  other arithmetic  27 us (9%)
  between operations  14.9 us (5%)
  matrix products  6.26 us (2%)
  local copies, waits for them, and re-layouts  5.8 us (2%)
  starting transfers between devices  4.5 us (1%)
    unnamed x3, waiting for transfers between devices  122 us
    psum x1, blocking collectives, per_device(): factor_gram, targets = lax.psum((factor_gram, targets), 'col')  82.2 us
    all_gather x1, waiting for transfers between devices, per_device(): factor = lax.all_gather(smoothed, 'cuts', axis=0, tiled=True)  41.6 us
    another operation x3, other arithmetic, per_device(): lower_factor = jnp.linalg.cholesky(mix_gram * weight_gram)  6.52 us
    another operation x3, other arithmetic, per_device(): lower_next = jnp.linalg.cholesky(mix_gram * factor_gram)  6.52 us
  transfers between devices with their start and end apart: 4, of which 4 were waited for; matrix products, arithmetic and copies ran while one was open for 0% of the time, Pallas kernels for 0%

commit v1 on v0

--- a/solution.py
+++ b/solution.py
@@ -133,7 +133,10 @@
         tiled=True,
     )
     smoothed = smooth(portion.reshape(-1, planes, cells))
-    factor = lax.all_gather(smoothed, "cuts", axis=0, tiled=True)
+    n_dev = lax.axis_size("cuts")
+    parts = jnp.stack([smoothed for _ in range(n_dev)])
+    parts = lax.all_to_all(parts, "cuts", split_axis=0, concat_axis=0)
+    factor = jnp.concatenate(parts, axis=0)
     factor_flat = factor.reshape(ranks, planes * cells)
     factor_half = factor_flat.astype(jnp.bfloat16)
     factor_gram = jnp.dot(factor_flat, factor_flat.T, precision=highest)

time: 310 us -> 291 us (0.939)
  the two profiles are of different devices: /device:TPU:8 before, /device:TPU:128 now
where the time goes in v1:
time: 291 us; the launch traced here: 290 us
  waiting for transfers between devices  126 us (43%)
  blocking collectives  103 us (35%)
  other arithmetic  25.1 us (9%)
  between operations  14.9 us (5%)
  starting transfers between devices  10.1 us (3%)
  local copies, waits for them, and re-layouts  5.9 us (2%)
  matrix products  5.19 us (2%)
    unnamed x2, waiting for transfers between devices  124 us
    psum x1, blocking collectives, per_device(): factor_gram, targets = lax.psum((factor_gram, targets), 'col')  83.2 us
    all_to_all x1, blocking collectives, per_device(): parts = lax.all_to_all(parts, 'cuts', split_axis=0, concat_axis=0)  19.7 us
    ppermute x1, starting transfers between devices, extended_2(): lax.ppermute(head, axis, [((i + 1) % count, i) for i in range(ends)])  6.69 us
    another operation x3, other arithmetic, per_device(): lower_factor = jnp.linalg.cholesky(mix_gram * weight_gram)  6.52 us
    another operation x3, other arithmetic, per_device(): lower_next = jnp.linalg.cholesky(mix_gram * factor_gram)  6.52 us
  transfers between devices with their start and end apart: 3, of which 3 were waited for; matrix products, arithmetic and copies ran while one was open for 0% of the time, Pallas kernels for 0%

profile of v1, /device:TPU:128, one launch (start us, length us, event | category | flops | bytes accessed | tf_op | source)
XLA Modules:
  0.0 290.5 jit_solution(15451912496171217994)
XLA Ops:
  7.2 1.1 fusion.59
  8.7 5.8 %cholesky.44 = f32[64,64]{1,0:T(8,128)S(1)} custom-call(f32[64,64]{1,0:T(8,128)S(1)} %fusion.45), custom_call_target="Cholesky" | custom-call | tf_op jit(solution)/shard_map/jit(cholesky)/cholesky | solution.py:120
  14.5 0.6 compare_reduce_fusion.1
  15.2 0.7 fusion.36
  15.8 4.9 %custom-call.16 = f32[1,64,64]{1,2,0:T(8,128)S(1)} custom-call(f32[1,64,64]{2,1,0:T(8,128)S(1)} %fusion.36), custom_call_target="InvertDiagBlocksLowerTriangular" | custom-call | tf_op jit(solution)/shard_map/jit(_cho_solve)/triangular_solve | solution.py:125
  21.3 1.2 copy.20
  22.5 1.3 fusion.60
  23.8 0.7 copy-done.2
  24.5 0.6 dynamic-slice
  26.0 123.8 %all-reduce.16.cloned.1.call-done = f32[64,4096]{1,0:T(8,128)} async-done(((f32[64,4096]{1,0:T(8,128)}), f32[64,4096]{1,0:T(8,128)}) %all-reduce.16.cloned.1.call-update) | async-done | bytes 1048592
  149.8 0.9 constant_dynamic-slice_fusion
  150.8 3.4 %collective-permute-start = (f32[4,3,1024]{2,1,0:T(4,128)S(1)}, f32[4,3,1024]{2,1,0:T(4,128)S(1)}, u32[]{:S(2)}, u32[]{:S(2)}) collective-permute-start(f32[4,3,1024]{2,1,0:T(4,128)S(1)} %get-tuple-element.11), channel_id=1, source_target_pairs={{0,1},{1,2},{2,3},{3,4},{4,5},{5,6},{6,7},{7,8},{8,9},{9,10},{10,1... | collective-permute-start | bytes 147464 | tf_op jit(solution)/shard_map/ppermute | solution.py:24
  154.2 6.7 %collective-permute-start.1 = (f32[4,3,1024]{2,1,0:T(4,128)S(1)}, f32[4,3,1024]{2,1,0:T(4,128)S(1)}, u32[]{:S(2)}, u32[]{:S(2)}) collective-permute-start(f32[4,3,1024]{2,1,0:T(4,128)S(1)} %get-tuple-element.12), channel_id=1, source_target_pairs={{1,0},{2,1},{3,2},{4,3},{5,4},{6,5},{7,6},{8,7},{9,8},{10,9},{11,1... | collective-permute-start | bytes 147464 | tf_op jit(solution)/shard_map/ppermute | solution.py:26
  161.3 2.1 collective-permute-done.1
  164.5 19.7 %all_to_all.5 = f32[16,4,4,1024]{3,2,1,0:T(4,128)S(1)} all-to-all(f32[16,4,4,1024]{3,2,1,0:T(4,128)S(1)} %stack.2), channel_id=1, replica_groups=mesh['cuts'=16,'col'=16] {'cuts'}, dimensions={0} | all-to-all | bytes 2097152 | tf_op jit(solution)/shard_map/all_to_all | solution.py:138
  184.8 0.6 copy.21
  185.4 1.0 fusion.61
  186.4 83.2 %all-reduce.13 = (f32[64,64]{0,1:T(8,128)S(1)}, f32[64]{0:T(128)S(1)}) all-reduce(f32[64,64]{0,1:T(8,128)S(1)} %fusion.61, f32[64]{0:T(128)S(1)} %fusion.1), channel_id=1, replica_groups=mesh['cuts'=16,'col'=16] {'col'}, use_global_device_ids=true, to_apply=%region_3.5 | all-reduce | flops 4160 | bytes 33280 | tf_op jit(solution)/shard_map/psum | solution.py:150
  269.7 5.8 %cholesky.55 = f32[64,64]{1,0:T(8,128)S(1)} custom-call(f32[64,64]{1,0:T(8,128)S(1)} %fusion.41), custom_call_target="Cholesky" | custom-call | tf_op jit(solution)/shard_map/jit(cholesky)/cholesky | solution.py:151
  275.6 0.6 compare_reduce_fusion
  276.2 0.7 fusion.37
  276.9 4.9 %custom-call.17 = f32[1,64,64]{1,2,0:T(8,128)S(1)} custom-call(f32[1,64,64]{2,1,0:T(8,128)S(1)} %fusion.37), custom_call_target="InvertDiagBlocksLowerTriangular" | custom-call | tf_op jit(solution)/shard_map/jit(_cho_solve)/triangular_solve | solution.py:152
  281.9 0.7 fusion.38
  282.6 1.0 copy.25
  (38 shorter events, 3.6 us)
Async XLA Ops:
  7.2 1.1 copy-start
  7.2 142.6 %all-reduce.16.cloned.1.call-start = ((), (), s32[]{:S(2)}) async-start(), calls=%async_computation.1 | async-start | bytes 2097152
  15.2 5.6 %copy-start.1 = (f32[64,64]{1,0:T(8,128)S(1)}, f32[64,64]{1,0:T(8,128)}, u32[]{:S(2)}) copy-start(f32[64,64]{1,0:T(8,128)} %param.6) | copy-start | bytes 49156
  23.8 0.7 copy-start.2
  150.8 10.5 %collective-permute-start = (f32[4,3,1024]{2,1,0:T(4,128)S(1)}, f32[4,3,1024]{2,1,0:T(4,128)S(1)}, u32[]{:S(2)}, u32[]{:S(2)}) collective-permute-start(f32[4,3,1024]{2,1,0:T(4,128)S(1)} %get-tuple-element.11), channel_id=1, source_target_pairs={{0,1},{1,2},{2,3},{3,4},{4,5},{5,6},{6,7},{7,8},{8,9},{9,10},{10,1... | collective-permute-start | bytes 147464 | tf_op jit(solution)/shard_map/ppermute | solution.py:24
  154.2 9.2 %collective-permute-start.1 = (f32[4,3,1024]{2,1,0:T(4,128)S(1)}, f32[4,3,1024]{2,1,0:T(4,128)S(1)}, u32[]{:S(2)}, u32[]{:S(2)}) collective-permute-start(f32[4,3,1024]{2,1,0:T(4,128)S(1)} %get-tuple-element.12), channel_id=1, source_target_pairs={{1,0},{2,1},{3,2},{4,3},{5,4},{6,5},{7,6},{8,7},{9,8},{10,9},{11,1... | collective-permute-start | bytes 147464 | tf_op jit(solution)/shard_map/ppermute | solution.py:26
Sparse Core Ops, SparseCore 0:
  23.9 125.7 all-reduce.15
